TPU v7x, 32 devices: a whole 2x2x4 slice. The times are simulated.
32 devices in a mesh: fsdp: 8 (over y, x, core), dp: 4 (over z).
Axes of the slice: x: 2, y: 2, z: 4, core: 2. Of those that a mesh axis runs over, the one named last changes fastest.
Arguments:
- tokens: bfloat16 [8, 1024, 1024], P('fsdp', 'dp'), may hold values from -6 to 6
- segment: int32 [8, 1024], P('fsdp', 'dp'), may hold values from 0 to 5, never falling along the last dimension, each value on 1 to 512 neighbouring positions
- grad_out: bfloat16 [8, 1024, 1024], P('fsdp', 'dp'), may hold values from -6 to 6
- w_query: bfloat16 [1024, 1024], P(('fsdp', 'dp')), may hold values from -0.1875 to 0.1875
- w_key: bfloat16 [1024, 1024], P(('fsdp', 'dp')), may hold values from -0.1875 to 0.1875
- w_value: bfloat16 [1024, 1024], P(('fsdp', 'dp')), may hold values from -0.1875 to 0.1875
- w_out: bfloat16 [1024, 1024], P(('fsdp', 'dp')), may hold values from -0.75 to 0.75
- b_query: bfloat16 [1024], P(('fsdp', 'dp')), may hold values from -3 to 3
- b_value: bfloat16 [1024], P(('fsdp', 'dp')), may hold values from -3 to 3
- b_out: bfloat16 [1024], P(('fsdp', 'dp')), may hold values from -2 to 2
- norm1_gain: bfloat16 [1024], P(('fsdp', 'dp')), may hold values from 0.5 to 1.5
- norm1_bias: bfloat16 [1024], P(('fsdp', 'dp')), may hold values from -2 to 2
- w_in: bfloat16 [1024, 4096], P(('fsdp', 'dp')), may hold values from -0.1875 to 0.1875
- b_in: bfloat16 [4096], P(('fsdp', 'dp')), may hold values from -3 to 3
- w_back: bfloat16 [4096, 1024], P(('fsdp', 'dp')), may hold values from -0.09375 to 0.09375
- b_back: bfloat16 [1024], P(('fsdp', 'dp')), may hold values from -2 to 2
- norm2_gain: bfloat16 [1024], P(('fsdp', 'dp')), may hold values from 0.5 to 1.5
- norm2_bias: bfloat16 [1024], P(('fsdp', 'dp')), may hold values from -2 to 2
Outputs:
- layer_out: bfloat16 [8, 1024, 1024], P('fsdp', 'dp')
- grad_tokens: float32 [8, 1024, 1024], P('fsdp', 'dp')
- grad_w_query: float32 [1024, 1024], P(('fsdp', 'dp'))
- grad_w_key: float32 [1024, 1024], P(('fsdp', 'dp'))
- grad_w_value: float32 [1024, 1024], P(('fsdp', 'dp'))
- grad_w_out: float32 [1024, 1024], P(('fsdp', 'dp'))
- grad_b_query: float32 [1024], P(('fsdp', 'dp'))
- grad_b_value: float32 [1024], P(('fsdp', 'dp'))
- grad_b_out: float32 [1024], P(('fsdp', 'dp'))
- grad_norm1_gain: float32 [1024], P(('fsdp', 'dp'))
- grad_norm1_bias: float32 [1024], P(('fsdp', 'dp'))
- grad_w_in: float32 [1024, 4096], P(('fsdp', 'dp'))
- grad_b_in: float32 [4096], P(('fsdp', 'dp'))
- grad_w_back: float32 [4096, 1024], P(('fsdp', 'dp'))
- grad_b_back: float32 [1024], P(('fsdp', 'dp'))
- grad_norm2_gain: float32 [1024], P(('fsdp', 'dp'))
- grad_norm2_bias: float32 [1024], P(('fsdp', 'dp'))
Inputs may be any that keep to these rules, and one draw needn't show every extreme that they name: segment numbers never fall along a sequence; a segment has at most 512 positions.
All inputs are finite; a program needn't handle non-finite values.
Results may differ from a plain program's by a relative error of at most 0.014.
Values may be sent and summed in bfloat16 or wider, within the bound.
No kernel may reach another device: no remote copies, remote signals or barrier semaphores. Data moves between devices by JAX's collectives and lax.ppermute only.
A program may use at most 192 MiB of HBM per device.

v0:
```python
from functools import partial

import jax
import jax.numpy as jnp
from jax import lax
from jax.sharding import PartitionSpec as P

HEAD_DIM = 64


norm_eps = 1e-05
neg_fill = -1000000000.0


def matmul(left, right):
    return jnp.dot(left, right, preferred_element_type=jnp.float32)


def matmul_t(left, right):
    return lax.dot_general(
        left, right, (((1,), (1,)), ((), ())), preferred_element_type=jnp.float32
    )


def outer_sum(left, right):
    return lax.dot_general(
        left, right, (((0,), (0,)), ((), ())), preferred_element_type=jnp.float32
    )


def col_sums(values):
    return jnp.sum(values.astype(jnp.float32), axis=0)


def normalize(rows_in, gain, shift):
    mean_rows = jnp.mean(rows_in, axis=-1, keepdims=True)
    centered = rows_in - mean_rows
    inverse = lax.rsqrt(jnp.mean(centered * centered, axis=-1, keepdims=True) + norm_eps)
    normed = centered * inverse
    return (normed * gain + shift, normed, inverse)


def normalize_back(grad_rows, normed, inverse, gain):
    scaled = grad_rows * gain
    return inverse * (
        scaled
        - jnp.mean(scaled, axis=-1, keepdims=True)
        - normed * jnp.mean(scaled * normed, axis=-1, keepdims=True)
    )


def to_pairs(flat_rows, seq_groups, seq_rows, head_pairs):
    return flat_rows.reshape(seq_groups, seq_rows, head_pairs, 2, -1).transpose(2, 0, 1, 3, 4)


def from_pairs(stacked):
    head_pairs, seq_groups, seq_rows, two_heads, head_size = stacked.shape
    return stacked.transpose(1, 2, 0, 3, 4).reshape(
        seq_groups * seq_rows, head_pairs * two_heads * head_size
    )


def body(
    tokens,
    segment,
    grad_out,
    w_query,
    w_key,
    w_value,
    w_out,
    b_query,
    b_value,
    b_out,
    norm1_gain,
    norm1_bias,
    w_in,
    b_in,
    w_back,
    b_back,
    norm2_gain,
    norm2_bias,
):
    attn_set = (
        lax.all_gather(w_query, ("fsdp", "dp"), axis=0, tiled=True),
        lax.all_gather(w_key, ("fsdp", "dp"), axis=0, tiled=True),
        lax.all_gather(w_value, ("fsdp", "dp"), axis=0, tiled=True),
        lax.all_gather(w_out, ("fsdp", "dp"), axis=0, tiled=True),
        lax.all_gather(b_query, ("fsdp", "dp"), axis=0, tiled=True),
        lax.all_gather(b_value, ("fsdp", "dp"), axis=0, tiled=True),
        lax.all_gather(b_out, ("fsdp", "dp"), axis=0, tiled=True),
        lax.all_gather(norm1_gain, ("fsdp", "dp"), axis=0, tiled=True),
        lax.all_gather(norm1_bias, ("fsdp", "dp"), axis=0, tiled=True),
    )
    q_weight, k_weight, v_weight, o_weight, q_bias, v_bias, o_bias, gain_one, shift_one = attn_set
    seq_groups, local_rows, model_width = tokens.shape
    head_pairs = model_width // (2 * HEAD_DIM)
    score_scale = HEAD_DIM ** (-0.5)
    flat_tokens = tokens.reshape(seq_groups * local_rows, model_width)
    wide_tokens = flat_tokens.astype(jnp.float32)
    query = (matmul(flat_tokens, q_weight) + q_bias.astype(jnp.float32)).astype(jnp.bfloat16)
    key_part = (
        matmul(flat_tokens, k_weight)
        .astype(jnp.bfloat16)
        .reshape(seq_groups, local_rows, model_width)
    )
    value_part = (
        (matmul(flat_tokens, v_weight) + v_bias.astype(jnp.float32))
        .astype(jnp.bfloat16)
        .reshape(seq_groups, local_rows, model_width)
    )
    seg_low = segment.astype(jnp.bfloat16)
    key_all, value_all, seg_all = (
        lax.all_gather(key_part, "dp", axis=1, tiled=True),
        lax.all_gather(value_part, "dp", axis=1, tiled=True),
        lax.all_gather(seg_low, "dp", axis=1, tiled=True),
    )
    full_len = key_all.shape[1]
    same_segment = seg_low[:, :, None] == seg_all[:, None, :]
    query_pairs = to_pairs(query, seq_groups, local_rows, head_pairs)
    key_pairs = to_pairs(
        key_all.reshape(seq_groups * full_len, model_width), seq_groups, full_len, head_pairs
    )
    value_pairs = to_pairs(
        value_all.reshape(seq_groups * full_len, model_width), seq_groups, full_len, head_pairs
    )

    def pair_scores(query_pair, key_pair):
        raw = (
            jnp.einsum("gqhe,gkhe->ghqk", query_pair, key_pair, preferred_element_type=jnp.float32)
            * score_scale
        )
        return jnp.where(same_segment[:, None], raw, neg_fill)

    def attend(pair_items):
        query_pair, key_pair, value_pair = pair_items
        scores = pair_scores(query_pair, key_pair)
        top_score = jnp.max(scores, axis=-1, keepdims=True)
        expo = jnp.exp(scores - top_score)
        total = jnp.sum(expo, axis=-1, keepdims=True)
        soft_low = (expo / total).astype(jnp.bfloat16)
        mixed_pair = jnp.einsum(
            "ghqk,gkhe->gqhe", soft_low, value_pair, preferred_element_type=jnp.float32
        )
        return (mixed_pair.astype(jnp.bfloat16), top_score[..., 0] + jnp.log(total[..., 0]))

    def attend_back(pair_items):
        query_pair, key_pair, value_pair, log_total, grad_pair = pair_items
        scores = pair_scores(query_pair, key_pair)
        probs = jnp.exp(scores - log_total[..., None])
        grad_probs = jnp.einsum(
            "gqhe,gkhe->ghqk", grad_pair, value_pair, preferred_element_type=jnp.float32
        )
        grad_value_pair = jnp.einsum(
            "ghqk,gqhe->gkhe",
            probs.astype(jnp.bfloat16),
            grad_pair,
            preferred_element_type=jnp.float32,
        )
        grad_scores = (
            probs * (grad_probs - jnp.sum(grad_probs * probs, axis=-1, keepdims=True))
        ).astype(jnp.bfloat16)
        grad_query_pair = (
            jnp.einsum("ghqk,gkhe->gqhe", grad_scores, key_pair, preferred_element_type=jnp.float32)
            * score_scale
        )
        grad_key_pair = (
            jnp.einsum(
                "ghqk,gqhe->gkhe", grad_scores, query_pair, preferred_element_type=jnp.float32
            )
            * score_scale
        )
        return (grad_query_pair.astype(jnp.bfloat16), grad_key_pair, grad_value_pair)

    mixed_pairs, log_totals = lax.map(attend, (query_pairs, key_pairs, value_pairs))
    mixed = from_pairs(mixed_pairs)
    branch = matmul(mixed, o_weight) + o_bias.astype(jnp.float32)
    hidden, normed_one, inverse_one = normalize(
        wide_tokens + branch, gain_one.astype(jnp.float32), shift_one.astype(jnp.float32)
    )
    mlp_set = (
        lax.all_gather(w_in, ("fsdp", "dp"), axis=0, tiled=True),
        lax.all_gather(b_in, ("fsdp", "dp"), axis=0, tiled=True),
        lax.all_gather(w_back, ("fsdp", "dp"), axis=0, tiled=True),
        lax.all_gather(b_back, ("fsdp", "dp"), axis=0, tiled=True),
        lax.all_gather(norm2_gain, ("fsdp", "dp"), axis=0, tiled=True),
        lax.all_gather(norm2_bias, ("fsdp", "dp"), axis=0, tiled=True),
    )
    in_weight, in_bias, out_weight, out_bias, gain_two, shift_two = mlp_set
    hidden_low = hidden.astype(jnp.bfloat16)
    pre_act = matmul(hidden_low, in_weight) + in_bias.astype(jnp.float32)
    activated = jax.nn.gelu(pre_act, approximate=False).astype(jnp.bfloat16)
    mlp_out = matmul(activated, out_weight) + out_bias.astype(jnp.float32)
    result, normed_two, inverse_two = normalize(
        hidden + mlp_out, gain_two.astype(jnp.float32), shift_two.astype(jnp.float32)
    )
    layer_out = result.astype(jnp.bfloat16).reshape(tokens.shape)
    mlp_set = (
        lax.all_gather(w_in, ("fsdp", "dp"), axis=0, tiled=True),
        lax.all_gather(b_in, ("fsdp", "dp"), axis=0, tiled=True),
        lax.all_gather(w_back, ("fsdp", "dp"), axis=0, tiled=True),
        lax.all_gather(b_back, ("fsdp", "dp"), axis=0, tiled=True),
        lax.all_gather(norm2_gain, ("fsdp", "dp"), axis=0, tiled=True),
        lax.all_gather(norm2_bias, ("fsdp", "dp"), axis=0, tiled=True),
    )
    in_weight, in_bias, out_weight, out_bias, gain_two, shift_two = mlp_set
    grad_top = grad_out.reshape(seq_groups * local_rows, model_width).astype(jnp.float32)
    grad_res_two = normalize_back(grad_top, normed_two, inverse_two, gain_two.astype(jnp.float32))
    grad_gain_two = jnp.sum(grad_top * normed_two, axis=0)
    grad_shift_two = jnp.sum(grad_top, axis=0)
    grad_mlp = grad_res_two.astype(jnp.bfloat16)
    grad_out_bias = col_sums(grad_mlp)
    grad_out_weight = outer_sum(activated, grad_mlp)
    grad_act = matmul_t(grad_mlp, out_weight)
    gelu_pull = jax.vjp(partial(jax.nn.gelu, approximate=False), pre_act)[1]
    grad_pre = gelu_pull(grad_act)[0].astype(jnp.bfloat16)
    grad_in_bias = col_sums(grad_pre)
    grad_in_weight = outer_sum(hidden_low, grad_pre)
    grad_hidden = matmul_t(grad_pre, in_weight) + grad_res_two
    mlp_terms = (
        grad_in_weight,
        grad_in_bias,
        grad_out_weight,
        grad_out_bias,
        grad_gain_two,
        grad_shift_two,
    )
    mlp_grads = (
        lax.psum_scatter(mlp_terms[0], ("fsdp", "dp"), scatter_dimension=0, tiled=True),
        lax.psum_scatter(mlp_terms[1], ("fsdp", "dp"), scatter_dimension=0, tiled=True),
        lax.psum_scatter(mlp_terms[2], ("fsdp", "dp"), scatter_dimension=0, tiled=True),
        lax.psum_scatter(mlp_terms[3], ("fsdp", "dp"), scatter_dimension=0, tiled=True),
        lax.psum_scatter(mlp_terms[4], ("fsdp", "dp"), scatter_dimension=0, tiled=True),
        lax.psum_scatter(mlp_terms[5], ("fsdp", "dp"), scatter_dimension=0, tiled=True),
    )
    attn_set = (
        lax.all_gather(w_query, ("fsdp", "dp"), axis=0, tiled=True),
        lax.all_gather(w_key, ("fsdp", "dp"), axis=0, tiled=True),
        lax.all_gather(w_value, ("fsdp", "dp"), axis=0, tiled=True),
        lax.all_gather(w_out, ("fsdp", "dp"), axis=0, tiled=True),
        lax.all_gather(b_query, ("fsdp", "dp"), axis=0, tiled=True),
        lax.all_gather(b_value, ("fsdp", "dp"), axis=0, tiled=True),
        lax.all_gather(b_out, ("fsdp", "dp"), axis=0, tiled=True),
        lax.all_gather(norm1_gain, ("fsdp", "dp"), axis=0, tiled=True),
        lax.all_gather(norm1_bias, ("fsdp", "dp"), axis=0, tiled=True),
    )
    q_weight, k_weight, v_weight, o_weight, q_bias, v_bias, o_bias, gain_one, shift_one = attn_set
    grad_res_one = normalize_back(
        grad_hidden, normed_one, inverse_one, gain_one.astype(jnp.float32)
    )
    grad_gain_one = jnp.sum(grad_hidden * normed_one, axis=0)
    grad_shift_one = jnp.sum(grad_hidden, axis=0)
    grad_branch = grad_res_one.astype(jnp.bfloat16)
    grad_o_bias = col_sums(grad_branch)
    grad_o_weight = outer_sum(mixed, grad_branch)
    grad_mixed = matmul_t(grad_branch, o_weight).astype(jnp.bfloat16)
    grad_mixed_pairs = to_pairs(grad_mixed, seq_groups, local_rows, head_pairs)
    grad_q_pairs, grad_k_pairs, grad_v_pairs = lax.map(
        attend_back, (query_pairs, key_pairs, value_pairs, log_totals, grad_mixed_pairs)
    )
    grad_query = from_pairs(grad_q_pairs)
    grad_k_whole = from_pairs(grad_k_pairs).reshape(seq_groups, full_len, model_width)
    grad_v_whole = from_pairs(grad_v_pairs).reshape(seq_groups, full_len, model_width)
    grad_key, grad_value = (
        lax.psum_scatter(
            grad_k_whole.astype(jnp.bfloat16), "dp", scatter_dimension=1, tiled=True
        ).astype(jnp.float32),
        lax.psum_scatter(
            grad_v_whole.astype(jnp.bfloat16), "dp", scatter_dimension=1, tiled=True
        ).astype(jnp.float32),
    )
    grad_key = grad_key.astype(jnp.bfloat16).reshape(seq_groups * local_rows, model_width)
    grad_value = grad_value.astype(jnp.bfloat16).reshape(seq_groups * local_rows, model_width)
    grad_q_bias = col_sums(grad_query)
    grad_v_bias = col_sums(grad_value)
    grad_q_weight = outer_sum(flat_tokens, grad_query)
    grad_k_weight = outer_sum(flat_tokens, grad_key)
    grad_v_weight = outer_sum(flat_tokens, grad_value)
    grad_input = (
        grad_res_one
        + matmul_t(grad_query, q_weight)
        + matmul_t(grad_key, k_weight)
        + matmul_t(grad_value, v_weight)
    )
    attn_terms = (
        grad_q_weight,
        grad_k_weight,
        grad_v_weight,
        grad_o_weight,
        grad_q_bias,
        grad_v_bias,
        grad_o_bias,
        grad_gain_one,
        grad_shift_one,
    )
    attn_grads = (
        lax.psum_scatter(attn_terms[0], ("fsdp", "dp"), scatter_dimension=0, tiled=True),
        lax.psum_scatter(attn_terms[1], ("fsdp", "dp"), scatter_dimension=0, tiled=True),
        lax.psum_scatter(attn_terms[2], ("fsdp", "dp"), scatter_dimension=0, tiled=True),
        lax.psum_scatter(attn_terms[3], ("fsdp", "dp"), scatter_dimension=0, tiled=True),
        lax.psum_scatter(attn_terms[4], ("fsdp", "dp"), scatter_dimension=0, tiled=True),
        lax.psum_scatter(attn_terms[5], ("fsdp", "dp"), scatter_dimension=0, tiled=True),
        lax.psum_scatter(attn_terms[6], ("fsdp", "dp"), scatter_dimension=0, tiled=True),
        lax.psum_scatter(attn_terms[7], ("fsdp", "dp"), scatter_dimension=0, tiled=True),
        lax.psum_scatter(attn_terms[8], ("fsdp", "dp"), scatter_dimension=0, tiled=True),
    )
    return (
        layer_out,
        grad_input.reshape(tokens.shape),
        attn_grads[0],
        attn_grads[1],
        attn_grads[2],
        attn_grads[3],
        attn_grads[4],
        attn_grads[5],
        attn_grads[6],
        attn_grads[7],
        attn_grads[8],
        mlp_grads[0],
        mlp_grads[1],
        mlp_grads[2],
        mlp_grads[3],
        mlp_grads[4],
        mlp_grads[5],
    )


def solution(mesh):
    placed = (
        P("fsdp", "dp", None),
        P("fsdp", "dp"),
        P("fsdp", "dp", None),
        P(("fsdp", "dp"), None),
        P(("fsdp", "dp"), None),
        P(("fsdp", "dp"), None),
        P(("fsdp", "dp"), None),
        P(("fsdp", "dp")),
        P(("fsdp", "dp")),
        P(("fsdp", "dp")),
        P(("fsdp", "dp")),
        P(("fsdp", "dp")),
        P(("fsdp", "dp"), None),
        P(("fsdp", "dp")),
        P(("fsdp", "dp"), None),
        P(("fsdp", "dp")),
        P(("fsdp", "dp")),
        P(("fsdp", "dp")),
    )
    return jax.shard_map(
        body,
        mesh=mesh,
        in_specs=placed,
        out_specs=(
            P("fsdp", "dp", None),
            P("fsdp", "dp", None),
            P(("fsdp", "dp"), None),
            P(("fsdp", "dp"), None),
            P(("fsdp", "dp"), None),
            P(("fsdp", "dp"), None),
            P(("fsdp", "dp")),
            P(("fsdp", "dp")),
            P(("fsdp", "dp")),
            P(("fsdp", "dp")),
            P(("fsdp", "dp")),
            P(("fsdp", "dp"), None),
            P(("fsdp", "dp")),
            P(("fsdp", "dp"), None),
            P(("fsdp", "dp")),
            P(("fsdp", "dp")),
            P(("fsdp", "dp")),
        ),
        check_vma=False,
    )
```

profile of v0, /device:TPU:0, one launch (start us, length us, event | category | flops | bytes accessed | tf_op | source)
XLA Modules:
  0.0 2017.0 jit_solution(14151019845585605851)
XLA Ops:
  16.2 42.3 %all-reduce.18 = (bf16[1024]{0:T(1024)(128)(2,1)S(1)}, bf16[1024]{0:T(1024)(128)(2,1)S(1)}, bf16[1024]{0:T(1024)(128)(2,1)S(1)}, bf16[1024]{0:T(1024)(128)(2,1)S...) all-reduce(bf16[1024]{0:T(1024)(128)(2,1)S(1)} %dynamic-update-slic, ...), channel_id=1, replica_groups=mesh['fsdp'=8,'dp'=4] {'fsdp','dp'}, use_global_device_ids=true, to_apply=%add | all-reduce | flops 8192 | bytes 32768
  58.5 11.5 all-gather.12.cloned.1.call-done
  70.0 3.3 fusion.62
  73.4 55.0 %all-gather.16.cloned.1.call-done = bf16[1024,1024]{1,0:T(8,128)(2,1)} async-done(((bf16[32,1024]{1,0:T(8,128)(2,1)}), bf16[1024,1024]{1,0:T(8,128)(2,1)}) %all-gather.16.cloned.1.call-update) | async-done | bytes 2097168 | tf_op jit(solution)/shard_map/all_gather | solution.py:85
  128.4 3.1 convolution_convert_fusion.2
  133.7 66.4 %all-gather.2 = bf16[32,1,128]{2,1,0:T(2,128)(2,1)S(1)} all-gather(bf16[1,1,128]{2,1,0:T(2,128)(2,1)S(1)} %bitcast.244), channel_id=1, replica_groups=mesh['fsdp'=8,'dp'=4] {'fsdp','dp'}, dimensions={0}, use_global_device_ids=true | all-gather | bytes 8448 | tf_op jit(solution)/shard_map/all_gather | solution.py:182
  200.2 8.3 all_gather.65
  208.5 2.3 fusion.63
  211.8 21.3 %all-gather.24.cloned.1.call-done = bf16[1024,1024]{1,0:T(8,128)(2,1)} async-done(((bf16[256,1024]{1,0:T(8,128)(2,1)}), bf16[1024,1024]{1,0:T(8,128)(2,1)}) %all-gather.24.cloned.1.call-update) | async-done | bytes 2097168 | tf_op jit(solution)/shard_map/all_gather | solution.py:114
  233.2 3.9 copy.56
  237.1 42.5 %all-gather.26.cloned.1.call-done = bf16[1024,1024]{1,0:T(8,128)(2,1)} async-done(((bf16[256,1024]{1,0:T(8,128)(2,1)}), bf16[1024,1024]{1,0:T(8,128)(2,1)}) %all-gather.26.cloned.1.call-update) | async-done | bytes 2097168 | tf_op jit(solution)/shard_map/all_gather | solution.py:113
  279.6 2.9 copy.58
  282.5 32.9 %while.28 = (s32[]{:T(128)}, bf16[8,1,256,2,64]{2,4,3,1,0:T(8,128)(2,1)S(1)}, f32[8,1,2,256]{3,2,1,0:T(2,128)S(1)}, bf16[8,1,1024,2,64]{2,4,3,1,0:T(8,128)(2,1)}...) while((s32[]{:T(128)}, ...), condition=%wide.region_3.4_spmd.clone, body=%wide.region_0.3_spmd.clone.sunk | while | flops 140803584 | bytes 8016481 | solution.py:174
  315.5 22.2 %all-gather.18.cloned.1.call-done = bf16[1024,1024]{1,0:T(8,128)(2,1)} async-done(((bf16[32,1024]{1,0:T(8,128)(2,1)}), bf16[1024,1024]{1,0:T(8,128)(2,1)}) %all-gather.18.cloned.1.call-update) | async-done | bytes 2097168 | tf_op jit(solution)/shard_map/all_gather | solution.py:87
  337.7 2.4 fusion.94
  340.4 76.2 %all-gather.20.cloned.1.call-done = bf16[1024,4096]{1,0:T(8,128)(2,1)} async-done(((bf16[32,4096]{1,0:T(8,128)(2,1)}), bf16[1024,4096]{1,0:T(8,128)(2,1)}) %all-gather.20.cloned.1.call-update) | async-done | bytes 8388624 | tf_op jit(solution)/shard_map/all_gather | solution.py:181
  416.6 16.2 multiply_convert_fusion.1
  432.7 62.5 %all-gather.22.cloned.1.call-done = bf16[4096,1024]{1,0:T(8,128)(2,1)} async-done(((bf16[128,1024]{1,0:T(8,128)(2,1)}), bf16[4096,1024]{1,0:T(8,128)(2,1)}) %all-gather.22.cloned.1.call-update) | async-done | bytes 8388624 | tf_op jit(solution)/shard_map/all_gather | solution.py:183
  495.2 6.5 fusion.95
  503.8 12.0 convert_reduce_fusion
  515.9 2.7 multiply_reduce_fusion.1
  520.8 71.1 %while.29 = (s32[]{:T(128)}, bf16[8,1,256,2,64]{2,4,3,1,0:T(8,128)(2,1)S(1)}, bf16[8,1,1024,2,64]{2,4,3,1,0:T(8,128)(2,1)}, bf16[8,1,1024,2,64]{2,4,3,1,0:T(8,12...) while((s32[]{:T(128)}, ...), condition=%wide.region_14.15_spmd.clone, body=%wide.region_12.14_spmd.clone.sunk | while | flops 340721152 | bytes 18433656 | solution.py:257
  524.6 1.9 fusion.148
  533.5 1.9 fusion.148
  542.4 1.9 fusion.148
  554.5 1.9 fusion.149
  572.3 1.9 fusion.149
  590.0 1.9 fusion.149
  592.8 2.6 convolution_bitcast_fusion.3
  595.5 5.6 copy.70
  601.1 3.7 fusion.80
  604.9 29.4 %reduce-scatter.15.cloned.1.call-done = bf16[1,256,1024]{1,2,0:T(8,128)(2,1)} async-done(((bf16[1,1024,1024]{1,2,0:T(8,128)(2,1)}), bf16[1,256,1024]{1,2,0:T(8,128)(2,1)}) %reduce-scatter.15.cloned.1.call-update) | async-done | bytes 524304 | tf_op jit(solution)/shard_map/reduce_scatter | solution.py:264
  634.3 3.7 convolution_bitcast_fusion.2
  638.0 5.4 copy.72
  643.5 35.9 %reduce-scatter.17.cloned.1.call-done = bf16[1,256,1024]{1,2,0:T(8,128)(2,1)} async-done(((bf16[1,1024,1024]{1,2,0:T(8,128)(2,1)}), bf16[1,256,1024]{1,2,0:T(8,128)(2,1)}) %reduce-scatter.17.cloned.1.call-update) | async-done | bytes 524304 | tf_op jit(solution)/shard_map/reduce_scatter | solution.py:267
  679.3 3.7 convolution_bitcast_fusion.1
  683.0 5.3 copy.74
  688.4 9.8 fusion.89
  699.5 9.7 fusion.83
  710.6 3.3 convolution_add_fusion.3
  714.2 41.2 %all-reduce.17 = (f32[1024]{0:T(1024)S(1)}, f32[1024]{0:T(1024)S(1)}, f32[1024]{0:T(1024)S(1)}, f32[1024]{0:T(1024)S(1)}, f32[1024]{0:T(1024)S(1)}, /*index=5*/f...) all-reduce(f32[1024]{0:T(1024)S(1)} %reduce_sum.182, ...), channel_id=10, replica_groups=mesh['fsdp'=8,'dp'=4] {'fsdp','dp'}, use_global_device_ids=true, to_apply=%region_22.23.clone | all-reduce | flops 12288 | bytes 98304
  760.6 2.6 convolution_add_fusion.2
  765.0 65.6 %reduce-scatter.25.cloned.1.call-done = f32[32,1024]{1,0:T(8,128)} async-done(((f32[1024,1024]{1,0:T(8,128)}), f32[32,1024]{1,0:T(8,128)}) %reduce-scatter.25.cloned.1.call-update) | async-done | bytes 131088
  830.6 150.7 %reduce-scatter.19.cloned.1.call-done = f32[32,1024]{1,0:T(8,128)} async-done(((f32[1024,1024]{1,0:T(8,128)}), f32[32,1024]{1,0:T(8,128)}) %reduce-scatter.19.cloned.1.call-update) | async-done | bytes 131088 | tf_op jit(solution)/shard_map/reduce_scatter | solution.py:299
  981.3 151.2 %reduce-scatter.27.cloned.1.call-done = f32[32,1024]{1,0:T(8,128)} async-done(((f32[1024,1024]{1,0:T(8,128)}), f32[32,1024]{1,0:T(8,128)}) %reduce-scatter.27.cloned.1.call-update) | async-done | bytes 131088
  1132.6 150.5 %reduce-scatter.29.cloned.1.call-done = f32[32,1024]{1,0:T(8,128)} async-done(((f32[1024,1024]{1,0:T(8,128)}), f32[32,1024]{1,0:T(8,128)}) %reduce-scatter.29.cloned.1.call-update) | async-done | bytes 131088
  1283.1 362.1 %reduce-scatter.21.cloned.1.call-done = f32[32,4096]{1,0:T(8,128)} async-done(((f32[1024,4096]{1,0:T(8,128)}), f32[32,4096]{1,0:T(8,128)}) %reduce-scatter.21.cloned.1.call-update) | async-done | bytes 524304 | tf_op jit(solution)/shard_map/reduce_scatter | solution.py:228
  1645.2 364.7 %reduce-scatter.23.cloned.1.call-done = f32[128,1024]{1,0:T(8,128)} async-done(((f32[4096,1024]{1,0:T(8,128)}), f32[128,1024]{1,0:T(8,128)}) %reduce-scatter.23.cloned.1.call-update) | async-done | bytes 524304 | tf_op jit(solution)/shard_map/reduce_scatter | solution.py:230
  (226 shorter events, 120.0 us)
Async XLA Ops:
  7.2 121.2 %copy-start.1 = (bf16[1,256,1024]{2,1,0:T(8,128)(2,1)S(1)}, bf16[1,256,1024]{2,1,0:T(8,128)(2,1)}, u32[]{:S(2)}) copy-start(bf16[1,256,1024]{2,1,0:T(8,128)(2,1)} %param.22) | copy-start | bytes 1572868
  7.2 62.8 %all-gather.12.cloned.1.call-start = ((), (), s32[]{:S(2)}) async-start(), calls=%async_computation.8 | async-start | bytes 2162688 | tf_op jit(solution)/shard_map/all_gather | solution.py:86
  7.9 120.4 %all-gather.16.cloned.1.call-start = ((), (), s32[]{:S(2)}) async-start(), calls=%async_computation.10 | async-start | bytes 2162688 | tf_op jit(solution)/shard_map/all_gather | solution.py:85
  8.7 199.8 %all-gather.14.cloned.1.call-start = ((), (), s32[]{:S(2)}) async-start(), calls=%async_computation.9 | async-start | bytes 2162688 | tf_op jit(solution)/shard_map/all_gather | solution.py:84
  9.4 223.7 %all-gather.24.cloned.1.call-start = ((), (), s32[]{:S(2)}) async-start(), calls=%async_computation.19 | async-start | bytes 2621440 | tf_op jit(solution)/shard_map/all_gather | solution.py:114
  58.5 75.2 %copy-start.12 = (s32[1,256]{1,0:T(1,128)S(1)}, s32[1,256]{1,0:T(1,128)}, u32[]{:S(2)}) copy-start(s32[1,256]{1,0:T(1,128)} %param.23) | copy-start | bytes 3076
  58.5 75.2 %copy-start.13 = (bf16[128]{0:T(256)(128)(2,1)S(1)}, bf16[128]{0:T(256)(128)(2,1)}, u32[]{:S(2)}) copy-start(bf16[128]{0:T(256)(128)(2,1)} %param.35) | copy-start | bytes 772
  73.3 206.3 %all-gather.26.cloned.1.call-start = ((), (), s32[]{:S(2)}) async-start(), calls=%async_computation.20 | async-start | bytes 2621440 | tf_op jit(solution)/shard_map/all_gather | solution.py:113
  131.5 206.2 %all-gather.18.cloned.1.call-start = ((), (), s32[]{:S(2)}) async-start(), calls=%async_computation.11 | async-start | bytes 2162688 | tf_op jit(solution)/shard_map/all_gather | solution.py:87
  132.1 284.5 %all-gather.20.cloned.1.call-start = ((), (), s32[]{:S(2)}) async-start(), calls=%async_computation.12 | async-start | bytes 8650752 | tf_op jit(solution)/shard_map/all_gather | solution.py:181
  132.8 362.4 %all-gather.22.cloned.1.call-start = ((), (), s32[]{:S(2)}) async-start(), calls=%async_computation.13 | async-start | bytes 8650752 | tf_op jit(solution)/shard_map/all_gather | solution.py:183
  133.6 500.8 %reduce-scatter.15.cloned.1.call-start = ((), (), s32[]{:S(2)}) async-start(), calls=%async_computation.14 | async-start | bytes 2621440 | tf_op jit(solution)/shard_map/reduce_scatter | solution.py:264
  315.5 22.2 %copy-start = (bf16[8,1,1024,2,64]{2,4,3,1,0:T(8,128)(2,1)}, bf16[8,1,1024,2,64]{2,4,3,1,0:T(8,128)(2,1)S(1)}, u32[]{:S(2)}) copy-start(bf16[8,1,1024,2,64]{2,4,3,1,0:T(8,128)(2,1)S(1)} %get-tuple-element.547) | copy-start | bytes 6291460
  315.5 117.3 %copy-start.6 = (bf16[8,1,256,2,64]{2,4,3,1,0:T(8,128)(2,1)}, bf16[8,1,256,2,64]{2,4,3,1,0:T(8,128)(2,1)S(1)}, u32[]{:S(2)}) copy-start(bf16[8,1,256,2,64]{2,4,3,1,0:T(8,128)(2,1)S(1)} %get-tuple-element.109) | copy-start | bytes 1572868
  495.2 6.8 copy-start.4
  502.6 13.3 slice-start
  503.8 12.0 copy-start.7
  503.8 12.1 slice-start.1
  515.9 2.8 copy-start.11
  515.9 3.1 copy-start.2
  591.9 87.4 %reduce-scatter.17.cloned.1.call-start = ((), (), s32[]{:S(2)}) async-start(), calls=%async_computation.15 | async-start | bytes 2621440 | tf_op jit(solution)/shard_map/reduce_scatter | solution.py:267
  592.5 238.1 %reduce-scatter.25.cloned.1.call-start = ((), (), s32[]{:S(2)}) async-start(), calls=%async_computation.21 | async-start | bytes 4325376
  601.1 380.3 %reduce-scatter.19.cloned.1.call-start = ((), (), s32[]{:S(2)}) async-start(), calls=%async_computation.16 | async-start | bytes 4325376 | tf_op jit(solution)/shard_map/reduce_scatter | solution.py:299
  604.9 527.7 %reduce-scatter.27.cloned.1.call-start = ((), (), s32[]{:S(2)}) async-start(), calls=%async_computation.22 | async-start | bytes 4325376
  643.4 639.7 %reduce-scatter.29.cloned.1.call-start = ((), (), s32[]{:S(2)}) async-start(), calls=%async_computation.23 | async-start | bytes 4325376
  688.4 956.8 %reduce-scatter.21.cloned.1.call-start = ((), (), s32[]{:S(2)}) async-start(), calls=%async_computation.17 | async-start | bytes 17301504 | tf_op jit(solution)/shard_map/reduce_scatter | solution.py:228
  698.3 1.2 copy-start.8
  698.3 1311.6 %reduce-scatter.23.cloned.1.call-start = ((), (), s32[]{:S(2)}) async-start(), calls=%async_computation.18 | async-start | bytes 17301504 | tf_op jit(solution)/shard_map/reduce_scatter | solution.py:230
  709.2 1.0 copy-start.5
  709.2 4.7 copy-start.3
  709.2 51.4 %copy-start.9 = (bf16[1,256,1024]{1,2,0:T(8,128)(2,1)S(1)}, bf16[1,256,1024]{1,2,0:T(8,128)(2,1)}, u32[]{:S(2)}) copy-start(bf16[1,256,1024]{1,2,0:T(8,128)(2,1)} %reduce-scatter.15.cloned.1.call-done) | copy-start | bytes 1572868
  713.9 49.3 %copy-start.10 = (bf16[1024,1024]{1,0:T(8,128)(2,1)S(1)}, bf16[1024,1024]{1,0:T(8,128)(2,1)}, u32[]{:S(2)}) copy-start(bf16[1024,1024]{1,0:T(8,128)(2,1)} %all-gather.12.cloned.1.call-done) | copy-start | bytes 6291460
Sparse Core Ops, SparseCore 0:
  10.9 59.0 all-gather.11
  73.0 55.3 all-gather.15
  131.3 55.2 all-gather.13
  188.6 44.5 all-gather.23
  235.1 44.4 all-gather.25
  282.4 55.2 all-gather.17
  340.6 75.9 all-gather.19
  419.5 75.6 all-gather.21
  592.1 42.2 reduce-scatter.14
  636.5 42.8 reduce-scatter.16
  682.2 148.3 reduce-scatter.24
  833.3 147.9 reduce-scatter.18
  984.2 148.3 reduce-scatter.26
  1135.3 147.7 reduce-scatter.28
  1285.8 359.3 reduce-scatter.20
  1648.0 361.9 reduce-scatter.22
where the time goes:
time: 2020 us
  waiting for transfers between devices  1610 us (80%)
  matrix products  183 us (9%)
  blocking collectives  158 us (8%)
  local copies, waits for them, and re-layouts  39.4 us (2%)
    unnamed x19, waiting for transfers between devices  372 us
    reduce_scatter x1, waiting for transfers between devices, body(): lax.psum_scatter(mlp_terms[2], ('fsdp', 'dp'), scatter_dimension=0, tiled...  365 us
    reduce_scatter x1, waiting for transfers between devices, body(): lax.psum_scatter(mlp_terms[0], ('fsdp', 'dp'), scatter_dimension=0, tiled...  362 us
    reduce_scatter x1, waiting for transfers between devices, body(): lax.psum_scatter(attn_terms[3], ('fsdp', 'dp'), scatter_dimension=0, tile...  151 us
    unnamed x2, blocking collectives  83.5 us
    all_gather x1, waiting for transfers between devices, body(): lax.all_gather(w_in, ('fsdp', 'dp'), axis=0, tiled=True)  76.2 us
    all_gather x1, blocking collectives, body(): lax.all_gather(b_in, ('fsdp', 'dp'), axis=0, tiled=True)  66.4 us
    all_gather x1, waiting for transfers between devices, body(): lax.all_gather(w_back, ('fsdp', 'dp'), axis=0, tiled=True)  62.5 us
  transfers between devices with their start and end apart: 16, of which 15 were waited for; matrix products, arithmetic and copies ran while one was open for 7% of the time, Pallas kernels for 0%

commit v1 on v0

v1 whole, which is shorter than its diff:
```python
from functools import partial

import jax
import jax.numpy as jnp
from jax import lax
from jax.experimental import pallas as pl
from jax.experimental.pallas import tpu as pltpu
from jax.sharding import PartitionSpec as P

HEAD_DIM = 64
PAIR = 2 * HEAD_DIM
AXES = ("fsdp", "dp")
NORM_EPS = 1e-05
NEG_FILL = -1000000000.0
F32 = jnp.float32
BF16 = jnp.bfloat16


def matmul(left, right):
    return jnp.dot(left, right, preferred_element_type=F32)


def matmul_t(left, right):
    return lax.dot_general(left, right, (((1,), (1,)), ((), ())), preferred_element_type=F32)


def outer_sum(left, right):
    return lax.dot_general(left, right, (((0,), (0,)), ((), ())), preferred_element_type=F32)


def col_sums(values):
    return jnp.sum(values.astype(F32), axis=0)


def normalize(rows_in, gain, shift):
    mean_rows = jnp.mean(rows_in, axis=-1, keepdims=True)
    centered = rows_in - mean_rows
    inverse = lax.rsqrt(jnp.mean(centered * centered, axis=-1, keepdims=True) + NORM_EPS)
    normed = centered * inverse
    return normed * gain + shift, normed, inverse


def normalize_back(grad_rows, normed, inverse, gain):
    scaled = grad_rows * gain
    return inverse * (
        scaled
        - jnp.mean(scaled, axis=-1, keepdims=True)
        - normed * jnp.mean(scaled * normed, axis=-1, keepdims=True)
    )


def head_lanes(rows, head):
    lane = lax.broadcasted_iota(jnp.int32, (rows, PAIR), 1)
    return (lane // HEAD_DIM) == head


def pair_scores(query, key, head, same):
    own = jnp.where(head_lanes(query.shape[0], head), query, jnp.zeros_like(query))
    raw = matmul_t(own, key) * (HEAD_DIM ** -0.5)
    return jnp.where(same, raw, NEG_FILL)


def attend_kernel(seg_q, seg_k, query, key, value, mixed, log_total):
    same = seg_q[...] == seg_k[...]
    rows = query.shape[0]
    outs, logs = [], []
    for head in range(2):
        scores = pair_scores(query[...], key[...], head, same)
        top = jnp.max(scores, axis=-1, keepdims=True)
        expo = jnp.exp(scores - top)
        total = jnp.sum(expo, axis=-1, keepdims=True)
        soft = (expo / total).astype(BF16)
        outs.append(matmul(soft, value[...]))
        logs.append(top + jnp.log(total))
    first = head_lanes(rows, 0)
    mixed[...] = jnp.where(first, outs[0], outs[1]).astype(BF16)
    log_total[...] = jnp.where(first, logs[0], logs[1])


def attend_back_kernel(
    seg_q, seg_k, query, key, value, log_total, grad_mixed, grad_query, grad_key, grad_value
):
    same = seg_q[...] == seg_k[...]
    rows = query.shape[0]
    dq, dk, dv = [], [], []
    for head in range(2):
        scores = pair_scores(query[...], key[...], head, same)
        probs = jnp.exp(scores - log_total[:, head * HEAD_DIM : head * HEAD_DIM + 1])
        grad_own = jnp.where(
            head_lanes(rows, head), grad_mixed[...], jnp.zeros_like(grad_mixed[...])
        )
        grad_probs = matmul_t(grad_own, value[...])
        row_sum = jnp.sum(grad_probs * probs, axis=-1, keepdims=True)
        grad_scores = (probs * (grad_probs - row_sum)).astype(BF16)
        dv.append(outer_sum(probs.astype(BF16), grad_mixed[...]))
        dq.append(matmul(grad_scores, key[...]))
        dk.append(outer_sum(grad_scores, query[...]))
    first = head_lanes(rows, 0)
    first_k = head_lanes(key.shape[0], 0)
    scale = HEAD_DIM ** -0.5
    grad_query[...] = (jnp.where(first, dq[0], dq[1]) * scale).astype(BF16)
    grad_key[...] = (jnp.where(first_k, dk[0], dk[1]) * scale).astype(BF16)
    grad_value[...] = jnp.where(first_k, dv[0], dv[1]).astype(BF16)


def attend(seg_q, seg_k, query, key, value):
    rows, width = query.shape
    full = key.shape[0]
    narrow = pl.BlockSpec((rows, PAIR), lambda p: (0, p))
    wide = pl.BlockSpec((full, PAIR), lambda p: (0, p))
    return pl.pallas_call(
        attend_kernel,
        grid=(width // PAIR,),
        in_specs=[
            pl.BlockSpec((rows, 1), lambda p: (0, 0)),
            pl.BlockSpec((1, full), lambda p: (0, 0)),
            narrow,
            wide,
            wide,
        ],
        out_specs=[narrow, narrow],
        out_shape=[
            jax.ShapeDtypeStruct((rows, width), BF16),
            jax.ShapeDtypeStruct((rows, width), F32),
        ],
        name="attend",
    )(seg_q, seg_k, query, key, value)


def attend_back(seg_q, seg_k, query, key, value, log_total, grad_mixed):
    rows, width = query.shape
    full = key.shape[0]
    narrow = pl.BlockSpec((rows, PAIR), lambda p: (0, p))
    wide = pl.BlockSpec((full, PAIR), lambda p: (0, p))
    return pl.pallas_call(
        attend_back_kernel,
        grid=(width // PAIR,),
        in_specs=[
            pl.BlockSpec((rows, 1), lambda p: (0, 0)),
            pl.BlockSpec((1, full), lambda p: (0, 0)),
            narrow,
            wide,
            wide,
            narrow,
            narrow,
        ],
        out_specs=[narrow, wide, wide],
        out_shape=[
            jax.ShapeDtypeStruct((rows, width), BF16),
            jax.ShapeDtypeStruct((full, width), BF16),
            jax.ShapeDtypeStruct((full, width), BF16),
        ],
        name="attend_back",
    )(seg_q, seg_k, query, key, value, log_total, grad_mixed)


def split_cols(block, width):
    rows, cols = block.shape
    parts = cols // width
    return block.reshape(rows, parts, width).transpose(1, 0, 2).reshape(rows * parts, width)


def gather_rows(block):
    count, width = block.shape
    whole = lax.all_gather(block, AXES, axis=0, tiled=True)
    return whole.reshape(-1, count, width)


def join_cols(stack, parts):
    devices, rows, width = stack.shape
    own = rows // parts
    return (
        stack.reshape(devices, parts, own, width)
        .transpose(0, 2, 1, 3)
        .reshape(devices * own, parts * width)
    )


def join_rows(stack):
    return stack.reshape(-1, stack.shape[-1])


def body(
    tokens,
    segment,
    grad_out,
    w_query,
    w_key,
    w_value,
    w_out,
    b_query,
    b_value,
    b_out,
    norm1_gain,
    norm1_bias,
    w_in,
    b_in,
    w_back,
    b_back,
    norm2_gain,
    norm2_bias,
):
    groups, rows, width = tokens.shape
    own = w_query.shape[0]
    ffn = w_in.shape[1]
    in_parts = ffn // width
    own_ffn = w_back.shape[0]
    vectors = (b_query, b_value, b_out, norm1_gain, norm1_bias, b_back, norm2_gain, norm2_bias)
    count = len(vectors)

    flat = tokens.reshape(rows, width)
    wide_tokens = flat.astype(F32)
    small = jnp.concatenate(vectors + (b_in,))
    small_len = small.shape[0]
    small_rows = jnp.zeros((8, width), BF16).at[0, :small_len].set(small)

    tokens_all = lax.all_gather(flat, "dp", axis=0, tiled=True)
    seg_low = segment.astype(BF16)
    seg_all = lax.all_gather(seg_low, "dp", axis=1, tiled=True)
    seg_q = segment.reshape(rows, 1).astype(F32)
    seg_k = seg_all.astype(F32)

    attn = gather_rows(jnp.concatenate([w_query, w_key, w_value, w_out, small_rows]))
    q_weight, k_weight, v_weight, o_weight = (
        join_rows(attn[:, i * own : (i + 1) * own]) for i in range(4)
    )
    small_all = attn[:, 4 * own, :small_len].astype(F32)
    per = small_all[:, : count * own].reshape(-1, count, own).transpose(1, 0, 2).reshape(count, -1)
    q_bias, v_bias, o_bias, gain_one, shift_one, out_bias, gain_two, shift_two = (
        per[i] for i in range(count)
    )
    in_bias = small_all[:, count * own :].reshape(-1)

    mlp = gather_rows(jnp.concatenate([split_cols(w_in, width), w_back]))
    in_weight = join_cols(mlp[:, : own * in_parts], in_parts)
    out_weight = join_rows(mlp[:, own * in_parts :])

    query = (matmul(flat, q_weight) + q_bias).astype(BF16)
    key = matmul(tokens_all, k_weight).astype(BF16)
    value = (matmul(tokens_all, v_weight) + v_bias).astype(BF16)
    mixed, log_total = attend(seg_q, seg_k, query, key, value)

    branch = matmul(mixed, o_weight) + o_bias
    hidden, normed_one, inverse_one = normalize(wide_tokens + branch, gain_one, shift_one)
    hidden_low = hidden.astype(BF16)
    pre_act = matmul(hidden_low, in_weight) + in_bias
    activated = jax.nn.gelu(pre_act, approximate=False).astype(BF16)
    mlp_out = matmul(activated, out_weight) + out_bias
    result, normed_two, inverse_two = normalize(hidden + mlp_out, gain_two, shift_two)
    layer_out = result.astype(BF16).reshape(tokens.shape)

    grad_top = grad_out.reshape(rows, width).astype(F32)
    grad_res_two = normalize_back(grad_top, normed_two, inverse_two, gain_two)
    grad_gain_two = jnp.sum(grad_top * normed_two, axis=0)
    grad_shift_two = jnp.sum(grad_top, axis=0)
    grad_mlp = grad_res_two.astype(BF16)
    grad_out_bias = col_sums(grad_mlp)
    grad_out_weight = outer_sum(activated, grad_mlp).astype(BF16)
    grad_act = matmul_t(grad_mlp, out_weight)
    gelu_pull = jax.vjp(partial(jax.nn.gelu, approximate=False), pre_act)[1]
    grad_pre = gelu_pull(grad_act)[0].astype(BF16)
    grad_in_bias = col_sums(grad_pre)
    grad_in_weight = outer_sum(hidden_low, grad_pre).astype(BF16)
    grad_hidden = matmul_t(grad_pre, in_weight) + grad_res_two

    devices = attn.shape[0]

    def by_device(grad):
        return grad.reshape(devices, -1, width)

    in_blocks = (
        grad_in_weight.reshape(devices, own, in_parts, width)
        .transpose(0, 2, 1, 3)
        .reshape(devices, own * in_parts, width)
    )
    mlp_blocks = jnp.concatenate([in_blocks, by_device(grad_out_weight)], axis=1)
    mlp_sum = lax.psum_scatter(join_rows(mlp_blocks), AXES, scatter_dimension=0, tiled=True)

    grad_res_one = normalize_back(grad_hidden, normed_one, inverse_one, gain_one)
    grad_gain_one = jnp.sum(grad_hidden * normed_one, axis=0)
    grad_shift_one = jnp.sum(grad_hidden, axis=0)
    grad_branch = grad_res_one.astype(BF16)
    grad_o_bias = col_sums(grad_branch)
    grad_o_weight = outer_sum(mixed, grad_branch).astype(BF16)
    grad_mixed = matmul_t(grad_branch, o_weight).astype(BF16)
    grad_query, grad_key, grad_value = attend_back(
        seg_q, seg_k, query, key, value, log_total, grad_mixed
    )
    grad_q_bias = col_sums(grad_query)
    grad_v_bias = col_sums(grad_value)
    grad_q_weight = outer_sum(flat, grad_query).astype(BF16)
    grad_k_weight = outer_sum(tokens_all, grad_key).astype(BF16)
    grad_v_weight = outer_sum(tokens_all, grad_value).astype(BF16)
    spread = (matmul_t(grad_key, k_weight) + matmul_t(grad_value, v_weight)).astype(BF16)
    spread_own = lax.psum_scatter(spread, "dp", scatter_dimension=0, tiled=True).astype(F32)
    grad_input = grad_res_one + matmul_t(grad_query, q_weight) + spread_own

    grad_vectors = jnp.stack(
        [
            grad_q_bias,
            grad_v_bias,
            grad_o_bias,
            grad_gain_one,
            grad_shift_one,
            grad_out_bias,
            grad_gain_two,
            grad_shift_two,
        ]
    )
    grad_small = jnp.concatenate(
        [
            grad_vectors.reshape(count, devices, own).transpose(1, 0, 2).reshape(devices, -1),
            grad_in_bias.reshape(devices, own_ffn),
        ],
        axis=1,
    ).astype(BF16)
    small_block = jnp.zeros((devices, 8, width), BF16).at[:, 0, :small_len].set(grad_small)
    attn_blocks = jnp.concatenate(
        [
            by_device(grad_q_weight),
            by_device(grad_k_weight),
            by_device(grad_v_weight),
            by_device(grad_o_weight),
            small_block,
        ],
        axis=1,
    )
    attn_sum = lax.psum_scatter(join_rows(attn_blocks), AXES, scatter_dimension=0, tiled=True)
    attn_sum = attn_sum.astype(F32)
    small_sum = attn_sum[4 * own, :small_len]
    vec = [small_sum[i * own : (i + 1) * own] for i in range(count)]
    grad_b_in = small_sum[count * own :]
    mlp_sum = mlp_sum.astype(F32)
    grad_w_in = (
        mlp_sum[: own * in_parts]
        .reshape(in_parts, own, width)
        .transpose(1, 0, 2)
        .reshape(own, ffn)
    )
    return (
        layer_out,
        grad_input.reshape(tokens.shape),
        attn_sum[:own],
        attn_sum[own : 2 * own],
        attn_sum[2 * own : 3 * own],
        attn_sum[3 * own : 4 * own],
        vec[0],
        vec[1],
        vec[2],
        vec[3],
        vec[4],
        grad_w_in,
        grad_b_in,
        mlp_sum[own * in_parts :],
        vec[5],
        vec[6],
        vec[7],
    )


def solution(mesh):
    act = P("fsdp", "dp", None)
    mat = P(AXES, None)
    vec = P(AXES)
    return jax.shard_map(
        body,
        mesh=mesh,
        in_specs=(act, P("fsdp", "dp"), act, mat, mat, mat, mat)
        + (vec,) * 5
        + (mat, vec, mat, vec, vec, vec),
        out_specs=(act, act, mat, mat, mat, mat) + (vec,) * 5 + (mat, vec, mat, vec, vec, vec),
        check_vma=False,
    )
```

time: 2020 us -> 980 us (0.49)
  waiting for transfers between devices: 1610 us -> 722 us
  blocking collectives: 158 us -> 12.7 us
  matrix products: 183 us -> 83.9 us
  local copies, waits for them, and re-layouts: 39.4 us -> 90 us
  Pallas kernels: 0 us -> 32.1 us
    reduce_scatter x5 -> x3, waiting for transfers between devices: 943 us -> 531 us  [the longest x1 356 us: body(): lax.psum_scatter(join_rows(mlp_blocks), AXES, scatter_dimension=0, tiled=...]
    unnamed x19 -> x6, waiting for transfers between devices: 372 us -> 0.78 us
    all_gather x8 -> x3, waiting for transfers between devices: 291 us -> 190 us  [the longest x2 155 us: gather_rows(): whole = lax.all_gather(block, AXES, axis=0, tiled=True)]
    dot_general x62 -> x6, matrix products: 127 us -> 35.7 us  [matmul(): return jnp.dot(left, right, preferred_element_type=F32)]
    unnamed x2 -> x0, blocking collectives: 83.5 us -> none
    all_gather x2 -> x1, blocking collectives: 74.6 us -> 12.7 us  [body(): seg_all = lax.all_gather(seg_low, 'dp', axis=1, tiled=True)]
    pallas_call x0 -> x2, Pallas kernels: none -> 32.1 us  [the longest x1 18.4 us: attend_back(): pl.pallas_call(attend_back_kernel, grid=(width // PAIR,), in_specs=[pl.Bl...]
    reshape x0 -> x5, local copies, waits for them, and re-layouts: none -> 27 us  [the longest x2 25.1 us: body(): grad_in_weight.reshape(devices, own, in_parts, width).transpose(0, 2, 1, 3)]
  transfers between devices with their start and end apart: 16 -> 6, of which waited for: 15 -> 5; matrix products, arithmetic and copies ran while one was open for 7% -> 10% of each run, Pallas kernels for 0% -> 1%
where the time goes in v1:
time: 980 us; the launch traced here: 973 us
  waiting for transfers between devices  722 us (74%)
  local copies, waits for them, and re-layouts  90 us (9%)
  matrix products  83.9 us (9%)
  Pallas kernels  32.1 us (3%)
  other arithmetic  16.5 us (2%)
  between operations  15 us (2%)
  blocking collectives  12.7 us (1%)
    reduce_scatter x1, waiting for transfers between devices, body(): lax.psum_scatter(join_rows(mlp_blocks), AXES, scatter_dimension=0, tiled=...  356 us
    reduce_scatter x1, waiting for transfers between devices, body(): lax.psum_scatter(join_rows(attn_blocks), AXES, scatter_dimension=0, tiled...  175 us
    all_gather x2, waiting for transfers between devices, gather_rows(): whole = lax.all_gather(block, AXES, axis=0, tiled=True)  155 us
    dot_general x6, matrix products, matmul(): return jnp.dot(left, right, preferred_element_type=F32)  35.7 us
    all_gather x1, waiting for transfers between devices, body(): tokens_all = lax.all_gather(flat, 'dp', axis=0, tiled=True)  35.4 us
    dot_general x6, matrix products, matmul_t(): lax.dot_general(left, right, (((1,), (1,)), ((), ())), preferred_element_...  30.8 us
    unnamed x62, local copies, waits for them, and re-layouts  25.6 us
    reshape x2, local copies, waits for them, and re-layouts, body(): grad_in_weight.reshape(devices, own, in_parts, width).transpose(0, 2, 1, 3)  25.1 us
  transfers between devices with their start and end apart: 6, of which 5 were waited for; matrix products, arithmetic and copies ran while one was open for 10% of the time, Pallas kernels for 1%

profile of v1, /device:TPU:0, one launch (start us, length us, event | category | flops | bytes accessed | tf_op | source)
XLA Modules:
  0.0 972.8 jit_solution(6538326609193663116)
XLA Ops:
  8.1 6.1 concatenate.34
  18.3 1.0 copy.71
  19.2 1.8 pad_maximum_fusion.1
  22.6 12.7 %all_gather.12 = bf16[1,1024]{1,0:T(2,128)(2,1)S(1)} all-gather(bf16[1,256]{1,0:T(2,128)(2,1)S(1)} %get-tuple-element.93), channel_id=1, replica_groups=mesh['fsdp'=8,'dp'=4] {'dp'}, dimensions={1}, use_global_device_ids=true | all-gather | bytes 2560 | tf_op jit(solution)/shard_map/all_gather | solution.py:219
  35.9 63.5 %all-gather.5.cloned.1.call-done = bf16[4352,1024]{1,0:T(8,128)(2,1)} async-done(((bf16[136,1024]{1,0:T(8,128)(2,1)}), bf16[4352,1024]{1,0:T(8,128)(2,1)}) %all-gather.5.cloned.1.call-update) | async-done | bytes 8912912 | tf_op jit(solution)/shard_map/all_gather | solution.py:165
  99.4 1.0 slice_convert_fusion
  101.4 5.6 fusion.54
  107.0 1.4 copy-done.3
  108.4 1.5 fusion.33.query
  109.9 35.4 %all-gather.9.cloned.1.call-done = bf16[1,1024,1024]{2,1,0:T(8,128)(2,1)} async-done(((bf16[1,256,1024]{2,1,0:T(8,128)(2,1)}), bf16[1,1024,1024]{2,1,0:T(8,128)(2,1)}) %all-gather.9.cloned.1.call-update) | async-done | bytes 2097168 | tf_op jit(solution)/shard_map/all_gather | solution.py:217
  145.3 6.0 convert_bitcast_fusion.key
  151.3 3.7 fusion.6.value
  155.0 13.7 %attend.1 = (bf16[256,1024]{1,0:T(8,128)(2,1)}, f32[256,1024]{1,0:T(8,128)}) custom-call(f32[256,1]{1,0:T(8,128)} %copy.53.seg_q, f32[1,1024]{1,0:T(1,128)} %convert_element_type.126.seg_k, bf16[256,1024]{1,0:T(8,128)(2,1)} %fusion.33.query, bf16[1024,1024]{1,0:T(8,128)(2,1)} %convert_bitcast_fusion.key, bf16[1024,1024]{1,0:T(8,128)(2,1)} %fusion.6.value), custom_call_target="tpu_custom_call" | custom-call | tf_op jit(solution)/shard_map/attend/pallas_call | solution.py:111
  168.8 2.0 fusion.58
  171.1 91.0 %all-gather.7.cloned.1.call-done = bf16[8192,1024]{1,0:T(8,128)(2,1)} async-done(((bf16[256,1024]{1,0:T(8,128)(2,1)}), bf16[8192,1024]{1,0:T(8,128)(2,1)}) %all-gather.7.cloned.1.call-update) | async-done | bytes 16777232 | tf_op jit(solution)/shard_map/all_gather | solution.py:165
  262.1 9.5 fusion.53
  271.6 8.1 copy.55
  279.7 12.1 %copy.68 = bf16[128,8,4,1024]{3,1,2,0:T(8,128)(2,1)} copy(bf16[128,8,4,1024]{3,2,1,0:T(4,128)(2,1)} %bitcast.135) | data formatting | bytes 16777216
  291.8 15.8 %multiply_convert_fusion = (bf16[256,4096]{1,0:T(8,128)(2,1)S(1)}, f32[256,4096]{1,0:T(8,128)}, f32[256,4096]{1,0:T(8,128)}) fusion(f32[4096]{0:T(1024)S(1)} %slice_bitcast_fusion, bf16[1024,4096]{1,0:T(8,128)(2,1)} %bitcast.140, f32[256,1024]{1,0:T(8,128)S(1)} %get-tuple-element.96, f32[1024]{0:T(1024)S(1)} %add.131, f32[1024]{0:T(1024)S(1)} %mul.129, ...), kind=kOutput, calls=%fused_computation.8 | convolution fusion | flops 2218000384 | bytes 19949568 | tf_op jit(solution)/shard_map/dot_general | solution.py:20
  307.7 6.7 fusion.59
  314.6 1.3 fusion.37
  316.3 13.0 %fusion.60 = (bf16[4096]{0:T(1024)(128)(2,1)S(1)}, bf16[256,4096]{1,0:T(8,128)(2,1)}) fusion(f32[256,4096]{1,0:T(8,128)} %get-tuple-element.71, f32[256,4096]{1,0:T(8,128)} %get-tuple-element.97, bf16[4096,1024]{1,0:T(8,128)(2,1)} %bitcast.146, f32[256,1024]{1,0:T(8,128)S(1)} %get-tuple-element.67), kind=kOutput, calls=%fused_computation.136 | convolution fusion | flops 2163470336 | bytes 19931136 | tf_op jit(solution)/shard_map/dot_general | solution.py:24
  329.3 4.5 multiply_reduce_fusion
  334.2 1.5 convolution_convert_fusion.4.grad_mixed
  335.7 18.4 %attend_back.1 = (bf16[256,1024]{1,0:T(8,128)(2,1)}, bf16[1024,1024]{1,0:T(8,128)(2,1)}, bf16[1024,1024]{1,0:T(8,128)(2,1)}) custom-call(f32[256,1]{1,0:T(8,128)} %copy.53.seg_q, f32[1,1024]{1,0:T(1,128)} %convert_element_type.126.seg_k, bf16[256,1024]{1,0:T(8,128)(2,1)} %fusion.33.query, bf16[1024,1024]{1,0:T(8,128)(2,1)} %convert_bitcast_fusion.key, ...), custom_call_target="tpu_custom_call" | custom-call | tf_op jit(solution)/shard_map/attend_back/pallas_call | solution.py:135
  354.1 4.7 fusion.61
  358.9 3.7 add_convert_fusion
  362.8 2.0 reduce.6
  365.8 2.0 convolution_convert_fusion.3
  367.8 1.5 constant_dynamic-update-slice_fusion.16
  369.3 2.5 fusion.17
  371.8 1.5 constant_dynamic-update-slice_fusion.15
  374.1 2.5 fusion.20
  376.6 1.6 constant_dynamic-update-slice_fusion.14
  378.9 1.5 constant_dynamic-update-slice_fusion.13
  380.4 0.9 pad_dynamic-update-slice_fusion
  381.6 7.4 convolution_convert_fusion.1
  388.9 14.6 %reshape.334 = bf16[32,32,4,1024]{3,2,1,0:T(4,128)(2,1)} reshape(bf16[1024,4096]{1,0:T(8,128)(2,1)} %convolution_convert_fusion.1) | data formatting | bytes 16777216 | tf_op jit(solution)/shard_map/reshape | solution.py:272
  403.5 10.5 %copy.59 = bf16[32,32,4,1024]{3,1,2,0:T(8,128)(2,1)} copy(bf16[32,32,4,1024]{3,2,1,0:T(4,128)(2,1)} %reshape.334) | data formatting | bytes 16777216 | tf_op jit(solution)/shard_map/reshape | solution.py:272
  414.0 2.4 convolution_convert_fusion
  416.4 1.0 copy-done
  417.4 6.7 pad_maximum_fusion
  424.2 3.4 fusion.26
  427.6 175.0 %reduce-scatter.6.cloned.1.call-done = bf16[136,1024]{1,0:T(8,128)(2,1)} async-done(((bf16[4352,1024]{1,0:T(8,128)(2,1)}), bf16[136,1024]{1,0:T(8,128)(2,1)}) %reduce-scatter.6.cloned.1.call-update) | async-done | bytes 278544 | tf_op jit(solution)/shard_map/reduce_scatter | solution.py:328
  602.6 1.0 convert_element_type.158
  604.7 1.7 fusion.56
  606.4 356.3 %reduce-scatter.8.cloned.1.call-done = bf16[256,1024]{1,0:T(8,128)(2,1)} async-done(((bf16[8192,1024]{1,0:T(8,128)(2,1)}), bf16[256,1024]{1,0:T(8,128)(2,1)}) %reduce-scatter.8.cloned.1.call-update) | async-done | bytes 524304 | tf_op jit(solution)/shard_map/reduce_scatter | solution.py:277
  962.8 1.9 fusion.55
  (115 shorter events, 14.5 us)
Async XLA Ops:
  7.2 92.2 %all-gather.5.cloned.1.call-start = ((), (), s32[]{:S(2)}) async-start(), calls=%async_computation.3 | async-start | bytes 9191424 | tf_op jit(solution)/shard_map/all_gather | solution.py:165
  16.7 0.7 copy-start.16
  17.5 127.9 %all-gather.9.cloned.1.call-start = ((), (), s32[]{:S(2)}) async-start(), calls=%async_computation.8 | async-start | bytes 2621440 | tf_op jit(solution)/shard_map/all_gather | solution.py:217
  18.2 243.9 %all-gather.7.cloned.1.call-start = ((), (), s32[]{:S(2)}) async-start(), calls=%async_computation.4 | async-start | bytes 17301504 | tf_op jit(solution)/shard_map/all_gather | solution.py:165
  21.0 403.2 %reduce-scatter.4.cloned.1.call-start = ((), (), s32[]{:S(2)}) async-start(), calls=%async_computation.5 | async-start | bytes 2621440 | tf_op jit(solution)/shard_map/reduce_scatter | solution.py:295
  101.4 6.9 copy-start.12
  107.0 1.4 copy-start.3
  107.0 61.8 %copy-start.1 = (bf16[32,32,1024]{2,1,0:T(8,128)(2,1)}, bf16[32,32,1024]{2,1,0:T(8,128)(2,1)S(1)}, u32[]{:S(2)}) copy-start(bf16[32,32,1024]{2,1,0:T(8,128)(2,1)S(1)} %get-tuple-element.74) | copy-start | bytes 6291460
  145.3 6.0 copy-start.13
  145.3 6.0 copy-start.17
  307.6 6.7 copy-start.8
  307.6 6.9 copy-start.4
  315.9 13.4 %slice-start = ((s8[8388608]{0:T(1024)(128)(4,1)}), s8[4194304]{0:T(1024)(128)(4,1)S(1)}, s32[]{:S(2)}) async-start(s8[8388608]{0:T(1024)(128)(4,1)} %bitcast.141), calls=%async_computation.9 | async-start | bytes 8388608
  316.3 13.0 %copy-start.6 = (f32[256,1024]{1,0:T(8,128)}, f32[256,1024]{1,0:T(8,128)S(1)}, u32[]{:S(2)}) copy-start(f32[256,1024]{1,0:T(8,128)S(1)} %get-tuple-element.67) | copy-start | bytes 3145732
  316.3 13.0 %slice-start.1 = ((s8[8388608]{0:T(1024)(128)(4,1)}), s8[4194304]{0:T(1024)(128)(4,1)S(1)}, s32[]{:S(2)}) async-start(s8[8388608]{0:T(1024)(128)(4,1)} %bitcast.141), calls=%async_computation.10 | async-start | bytes 8388608
  329.3 4.8 copy-start.2
  354.1 4.8 copy-start.10
  354.1 4.8 copy-start.14
  362.6 2.2 copy-start.5
  362.6 240.0 %reduce-scatter.6.cloned.1.call-start = ((), (), s32[]{:S(2)}) async-start(), calls=%async_computation.6 | async-start | bytes 9191424 | tf_op jit(solution)/shard_map/reduce_scatter | solution.py:328
  365.7 3.6 copy-start.18
  365.7 3.6 copy-start.19
  371.7 2.4 copy-start.11
  376.6 1.6 copy-start.15
  381.3 581.5 %reduce-scatter.8.cloned.1.call-start = ((), (), s32[]{:S(2)}) async-start(), calls=%async_computation.7 | async-start | bytes 17301504 | tf_op jit(solution)/shard_map/reduce_scatter | solution.py:277
  403.5 10.5 %copy-start.7 = (f32[256,1024]{1,0:T(8,128)S(1)}, f32[256,1024]{1,0:T(8,128)}, u32[]{:S(2)}) copy-start(f32[256,1024]{1,0:T(8,128)} %copy-done.6) | copy-start | bytes 3145732
  403.5 10.5 %copy-start.9 = (bf16[256,4096]{1,0:T(8,128)(2,1)S(1)}, bf16[256,4096]{1,0:T(8,128)(2,1)}, u32[]{:S(2)}) copy-start(bf16[256,4096]{1,0:T(8,128)(2,1)} %copy-done.8) | copy-start | bytes 6291460
  414.0 3.4 copy-start
Sparse Core Ops, SparseCore 0:
  17.6 81.7 all-gather.4
  101.0 44.2 all-gather.8
  148.9 113.1 all-gather.6
  362.7 41.8 reduce-scatter.3
  406.8 195.7 reduce-scatter.5
  604.7 357.9 reduce-scatter.7
